TPU v7x, 256 devices: a whole 4x4x8 slice. The times are simulated.
256 devices in a mesh: pipe: 8 (over x, core), seq: 8 (over z), tensor: 4 (over y).
Axes of the slice: x: 4, y: 4, z: 8, core: 2. Of those that a mesh axis runs over, the one named last changes fastest.
Arguments:
- hidden: bfloat16 [8, 1024, 14336], P('pipe', 'seq', 'tensor'), may hold values from -6 to 6
- down_weight: bfloat16 [8, 14336, 8192], P('pipe', 'tensor', 'seq'), may hold values from -0.046875 to 0.046875
- resid: bfloat16 [1024, 8192], P('tensor', 'seq'), may hold values from -42 to 42
- target: bfloat16 [1024, 8192], P('tensor', 'seq'), may hold values from -6 to 6
- gain: float32 [8192], P('seq'), may hold values from 0.1 to 1.9
- query_left: float32 [8, 8192, 32], P('pipe', 'seq'), may hold values from -0.0625 to 0.0625
- query_right: bfloat16 [8, 14336, 32], P('pipe', 'tensor'), may hold values from -0.046875 to 0.046875
- query_core: float32 [8, 1024], P('pipe'), may hold values from -6 to 6
- eigen: float32 [8, 1024], P('pipe'), may hold values from 0.1 to 10
- lengths: int32 [32], replicated, may hold values from 1 to 256, 1024 in all
Outputs:
- scores: float32 [32], P(('seq', 'tensor'))
All inputs are finite; a program needn't handle non-finite values.
Results may differ from a plain program's by a relative error of at most 0.0006.
Values may be sent and summed in bfloat16 or wider, within the bound.
No kernel may reach another device: no remote copies, remote signals or barrier semaphores. Data moves between devices by JAX's collectives and lax.ppermute only.
A program may use at most 64 MiB of HBM per device.

v0:
```python
import jax
import jax.numpy as jnp
from jax import lax
from jax.sharding import PartitionSpec as P

D = 8192


def per_device(
    hidden, down_weight, resid, target, gain, query_left, query_right, query_core, eigen, lengths
):
    tensor_count = lax.axis_size("tensor")
    gathered = lax.all_gather(hidden[0], "seq", axis=0, tiled=True)
    total_rows = gathered.shape[0]
    block_rows = total_rows // tensor_count
    weight = down_weight[0]
    right_partial = jnp.dot(gathered, query_right[0], preferred_element_type=jnp.float32)
    partial_value = lax.psum_scatter(
        jnp.dot(gathered, weight, preferred_element_type=jnp.float32).astype(jnp.bfloat16),
        "tensor",
        scatter_dimension=0,
        tiled=True,
    ).astype(jnp.float32)
    summed = lax.psum(partial_value, "pipe")
    stream = resid.astype(jnp.float32) + summed
    weighted_target = gain[None, :] * target.astype(jnp.float32)
    square_sum, inner = lax.psum(
        (jnp.sum(stream * stream, axis=1), jnp.sum(weighted_target * stream, axis=1)), "seq"
    )
    root = jnp.sqrt(square_sum / D + 1e-05)
    grad_stream = (
        weighted_target / root[:, None] - stream * (inner / (D * root * root * root))[:, None]
    )
    left_proj = jnp.dot(grad_stream, query_left[0], precision=lax.Precision.HIGHEST)
    right_proj = lax.psum_scatter(right_partial, "tensor", scatter_dimension=0, tiled=True)
    rank_width = left_proj.shape[1]
    outer = (left_proj[:, :, None] * right_proj[:, None, :]).reshape(
        block_rows, rank_width * rank_width
    )
    ends = jnp.cumsum(lengths)
    starts = ends - lengths
    token = lax.axis_index("tensor") * block_rows + jnp.arange(block_rows, dtype=jnp.int32)
    member = ((token[None, :] >= starts[:, None]) & (token[None, :] < ends[:, None])).astype(
        jnp.float32
    )
    partial_cores = jnp.dot(member, outer, precision=lax.Precision.HIGHEST)
    cores = lax.psum_scatter(partial_cores, ("seq", "tensor"), scatter_dimension=0, tiled=True)
    scaled = cores / eigen[0][None, :]
    score_term = jnp.sum(query_core[0][None, :] * scaled, axis=1)
    self_term = jnp.sum(cores * scaled, axis=1)
    score_total, self_total = lax.psum((score_term, self_term), "pipe")
    return score_total / jnp.sqrt(self_total + 1e-06)


def solution(mesh):
    placed = (
        P("pipe", "seq", "tensor"),
        P("pipe", "tensor", "seq"),
        P("tensor", "seq"),
        P("tensor", "seq"),
        P("seq"),
        P("pipe", "seq", None),
        P("pipe", "tensor", None),
        P("pipe", None),
        P("pipe", None),
        P(),
    )
    return jax.shard_map(
        per_device, mesh=mesh, in_specs=placed, out_specs=P(("seq", "tensor")), check_vma=False
    )
```

profile of v0, /device:TPU:1, one launch (start us, length us, event | category | flops | bytes accessed | tf_op | source)
XLA Modules:
  0.0 375.0 jit_solution(16374362809391073880)
XLA Ops:
  6.5 0.7 all-gather.3.cloned.1.call-update
  7.3 0.0 reduce-scatter.3.cloned.1.call-start
  7.3 90.0 %all-gather.3.cloned.1.call-done = bf16[1,1024,3584]{2,1,0:T(8,128)(2,1)} async-done(((bf16[1,128,3584]{2,1,0:T(8,128)(2,1)}), bf16[1,1024,3584]{2,1,0:T(8,128)(2,1)}) %all-gather.3.cloned.1.call-update) | async-done | bytes 7340048 | tf_op jit(solution)/shard_map/all_gather | solution.py:13
  97.3 13.3 %fusion.5 = bf16[1024,1024]{1,0:T(8,128)(2,1)} fusion(bf16[1,3584,1024]{2,1,0:T(8,128)(2,1)} %param.11, bf16[1,1024,3584]{2,1,0:T(8,128)(2,1)} %all-gather.3.cloned.1.call-done), kind=kOutput, calls=%fused_computation.5 | convolution fusion | flops 7517241344 | bytes 16777216 | tf_op jit(solution)/shard_map/dot_general | solution.py:19
  110.6 0.0 reduce-scatter.3.cloned.1.call-update
  110.6 0.0 reduce-scatter.5.cloned.1.call-start
  110.7 0.1 copy.15
  110.8 0.1 reduce-window.8
  110.8 0.1 reduce.2
  111.0 6.0 %fusion.2 = f32[1024,32]{0,1:T(8,128)} fusion(bf16[1,1024,3584]{2,1,0:T(8,128)(2,1)} %all-gather.3.cloned.1.call-done, bf16[1,3584,32]{1,2,0:T(8,128)(2,1)S(1)} %copy-done), kind=kOutput, calls=%fused_computation.2 | convolution fusion | flops 234881024 | bytes 7700480 | tf_op jit(solution)/shard_map/dot_general | solution.py:17
  116.9 0.0 reduce-scatter.5.cloned.1.call-update
  117.0 0.0 all-reduce.6.cloned.1.call-start
  117.0 24.6 %reduce-scatter.3.cloned.1.call-done = bf16[256,1024]{1,0:T(8,128)(2,1)} async-done(((bf16[1024,1024]{1,0:T(8,128)(2,1)}), bf16[256,1024]{1,0:T(8,128)(2,1)}) %reduce-scatter.3.cloned.1.call-update) | async-done | bytes 524304 | tf_op jit(solution)/shard_map/reduce_scatter | solution.py:18
  141.7 50.4 %all-reduce.7 = f32[256,1024]{1,0:T(8,128)S(1)} all-reduce(bf16[256,1024]{1,0:T(8,128)(2,1)} %reduce-scatter.3.cloned.1.call-done), channel_id=1, replica_groups=mesh['pipe'=8,'seq'=8,'tensor'=4] {'pipe'}, use_global_device_ids=true, to_apply=%region_2.0 | all-reduce | flops 262144 | bytes 1572864 | tf_op jit(solution)/shard_map/psum | solution.py:24
  192.1 0.4 multiply_reduce_fusion.1
  192.5 13.7 %all-reduce.1 = (f32[256]{0:T(256)S(1)}, f32[256]{0:T(256)S(1)}) all-reduce(f32[256]{0:T(256)S(1)} %get-tuple-element.6, f32[256]{0:T(256)S(1)} %get-tuple-element.5), channel_id=1, replica_groups=mesh['pipe'=8,'seq'=8,'tensor'=4] {'seq'}, use_global_device_ids=true, to_apply=%region_6.0 | all-reduce | flops 512 | bytes 4096 | tf_op jit(solution)/shard_map/psum | solution.py:27
  206.2 1.2 fusion.10
  207.4 0.0 reduce-scatter.5.cloned.1.call-done
  207.5 0.9 broadcast_multiply_fusion
  208.3 1.3 fusion.19
  209.7 0.6 dynamic-slice
  210.3 137.4 %all-reduce.6.cloned.1.call-done = f32[32,1024]{1,0:T(8,128)} async-done(((f32[32,1024]{1,0:T(8,128)}), f32[32,1024]{1,0:T(8,128)}) %all-reduce.6.cloned.1.call-update) | async-done | bytes 131088
  347.7 2.0 multiply_reduce_fusion.2
  349.7 16.9 %all-reduce.2 = (f32[1]{0:T(128)}, f32[1]{0:T(128)}) all-reduce(f32[1]{0:T(128)} %bitcast.6, f32[1]{0:T(128)} %bitcast.7), channel_id=1, replica_groups=mesh['pipe'=8,'seq'=8,'tensor'=4] {'pipe'}, use_global_device_ids=true, to_apply=%region_10.11 | all-reduce | flops 2 | bytes 16 | tf_op jit(solution)/shard_map/psum | solution.py:51
  (23 shorter events, 0.1 us)
Async XLA Ops:
  6.5 104.4 %copy-start = (bf16[1,3584,32]{1,2,0:T(8,128)(2,1)S(1)}, bf16[1,3584,32]{1,2,0:T(8,128)(2,1)}, u32[]{:S(2)}) copy-start(bf16[1,3584,32]{1,2,0:T(8,128)(2,1)} %param.16) | copy-start | bytes 688132
  6.5 90.8 %all-gather.3.cloned.1.call-start = ((), (), s32[]{:S(2)}) async-start(), calls=%async_computation.4 | async-start | bytes 8257536 | tf_op jit(solution)/shard_map/all_gather | solution.py:13
  7.3 103.4 %copy-start.6 = (s32[32]{0:T(128)S(1)}, s32[32]{0:T(128)}, u32[]{:S(2)}) copy-start(s32[32]{0:T(128)} %param.19) | copy-start | bytes 388
  7.3 134.4 %reduce-scatter.3.cloned.1.call-start = ((), (), s32[]{:S(2)}) async-start(), calls=%async_computation.2 | async-start | bytes 2621440 | tf_op jit(solution)/shard_map/reduce_scatter | solution.py:18
  110.6 81.5 %copy-start.1 = (bf16[256,1024]{1,0:T(8,128)(2,1)S(1)}, bf16[256,1024]{1,0:T(8,128)(2,1)}, u32[]{:S(2)}) copy-start(bf16[256,1024]{1,0:T(8,128)(2,1)} %param.13) | copy-start | bytes 1572868
  110.6 81.5 %copy-start.2 = (bf16[256,1024]{1,0:T(8,128)(2,1)S(1)}, bf16[256,1024]{1,0:T(8,128)(2,1)}, u32[]{:S(2)}) copy-start(bf16[256,1024]{1,0:T(8,128)(2,1)} %param.12) | copy-start | bytes 1572868
  110.6 81.5 %copy-start.3 = (f32[1024]{0:T(1024)S(1)}, f32[1024]{0:T(1024)}, u32[]{:S(2)}) copy-start(f32[1024]{0:T(1024)} %param.14) | copy-start | bytes 12292
  110.6 95.6 %copy-start.7 = (f32[1,1024,32]{1,2,0:T(8,128)S(1)}, f32[1,1024,32]{1,2,0:T(8,128)}, u32[]{:S(2)}) copy-start(f32[1,1024,32]{1,2,0:T(8,128)} %param.15) | copy-start | bytes 393220
  110.6 96.9 %reduce-scatter.5.cloned.1.call-start = ((), (), s32[]{:S(2)}) async-start(), calls=%async_computation.3 | async-start | bytes 163840 | tf_op jit(solution)/shard_map/reduce_scatter | solution.py:35
  116.9 92.8 %copy-start.8 = (u32[256]{0:T(256)S(1)}, u32[256]{0:T(256)}, u32[]{:S(2)}) copy-start(u32[256]{0:T(256)} %constant.28) | copy-start | bytes 3076
  116.9 230.7 %copy-start.4 = (f32[1,1024]{1,0:T(1,128)S(1)}, f32[1,1024]{1,0:T(1,128)}, u32[]{:S(2)}) copy-start(f32[1,1024]{1,0:T(1,128)} %param.17) | copy-start | bytes 12292
  116.9 230.7 %copy-start.5 = (f32[1,1024]{1,0:T(1,128)S(1)}, f32[1,1024]{1,0:T(1,128)}, u32[]{:S(2)}) copy-start(f32[1,1024]{1,0:T(1,128)} %param.18) | copy-start | bytes 12292
  117.0 230.7 %all-reduce.6.cloned.1.call-start = ((), (), s32[]{:S(2)}) async-start(), calls=%async_computation.5 | async-start | bytes 262144
Sparse Core Ops, SparseCore 0:
  9.1 88.1 all-gather.2
  110.7 30.8 reduce-scatter.2
  144.3 20.4 reduce-scatter.4
  209.8 137.8 all-reduce.5
where the time goes:
time: 375 us
  waiting for transfers between devices  253 us (67%)
  blocking collectives  81 us (22%)
  matrix products  21.7 us (6%)
  between operations  15.1 us (4%)
    unnamed x5, waiting for transfers between devices  138 us
    all_gather x1, waiting for transfers between devices, per_device(): gathered = lax.all_gather(hidden[0], 'seq', axis=0, tiled=True)  90 us
    psum x1, blocking collectives, per_device(): summed = lax.psum(partial_value, 'pipe')  50.4 us
    reduce_scatter x1, waiting for transfers between devices, per_device(): lax.psum_scatter(jnp.dot(gathered, weight, preferred_element_type=jnp.flo...  24.6 us
    psum x1, blocking collectives, per_device(): score_total, self_total = lax.psum((score_term, self_term), 'pipe')  16.9 us
    psum x1, blocking collectives, per_device(): lax.psum((jnp.sum(stream * stream, axis=1), jnp.sum(weighted_target * str...  13.7 us
    dot_general x1, matrix products, per_device(): jnp.dot(gathered, weight, preferred_element_type=jnp.float32)  13.3 us
  transfers between devices with their start and end apart: 4, of which 3 were waited for; matrix products, arithmetic and copies ran while one was open for 2% of the time, Pallas kernels for 0%

commit v1 on v0

--- a/solution.py
+++ b/solution.py
@@ -21,7 +21,7 @@
         scatter_dimension=0,
         tiled=True,
     ).astype(jnp.float32)
-    summed = lax.psum(partial_value, "pipe")
+    summed = jnp.sum(lax.all_gather(partial_value, "pipe"), axis=0)
     stream = resid.astype(jnp.float32) + summed
     weighted_target = gain[None, :] * target.astype(jnp.float32)
     square_sum, inner = lax.psum(

time: 375 us -> 389 us (1.037)
  waiting for transfers between devices: 253 us -> 310 us
  blocking collectives: 81 us -> 30.8 us
  other arithmetic: 3.46 us -> 9.97 us
    psum x1 -> x0, blocking collectives: 50.4 us -> none  [per_device(): summed = lax.psum(partial_value, 'pipe')]
    all_gather x0 -> x1, waiting for transfers between devices: none -> 46 us  [per_device(): summed = jnp.sum(lax.all_gather(partial_value, 'pipe'), axis=0)]
    reduce_scatter x1, waiting for transfers between devices: 24.6 us -> 31 us  [per_device(): lax.psum_scatter(jnp.dot(gathered, weight, preferred_element_type=jnp.flo...]
    reduce_sum x0 -> x1, other arithmetic: none -> 4.38 us  [per_device(): summed = jnp.sum(lax.all_gather(partial_value, 'pipe'), axis=0)]
    unnamed x5 -> x6, waiting for transfers between devices: 138 us -> 140 us
  transfers between devices with their start and end apart: 4 -> 5, of which waited for: 3 -> 5; matrix products, arithmetic and copies ran while one was open for 2% -> 3% of each run, Pallas kernels for 0% -> 0%
where the time goes in v1:
time: 389 us
  waiting for transfers between devices  310 us (80%)
  blocking collectives  30.8 us (8%)
  matrix products  21.7 us (6%)
  between operations  15.2 us (4%)
  other arithmetic  9.97 us (3%)
    unnamed x6, waiting for transfers between devices  140 us
    all_gather x1, waiting for transfers between devices, per_device(): gathered = lax.all_gather(hidden[0], 'seq', axis=0, tiled=True)  90 us
    all_gather x1, waiting for transfers between devices, per_device(): summed = jnp.sum(lax.all_gather(partial_value, 'pipe'), axis=0)  46 us
    reduce_scatter x1, waiting for transfers between devices, per_device(): lax.psum_scatter(jnp.dot(gathered, weight, preferred_element_type=jnp.flo...  31 us
    psum x1, blocking collectives, per_device(): score_total, self_total = lax.psum((score_term, self_term), 'pipe')  16.9 us
    psum x1, blocking collectives, per_device(): lax.psum((jnp.sum(stream * stream, axis=1), jnp.sum(weighted_target * str...  13.9 us
    dot_general x1, matrix products, per_device(): jnp.dot(gathered, weight, preferred_element_type=jnp.float32)  13.2 us
  transfers between devices with their start and end apart: 5, of which 5 were waited for; matrix products, arithmetic and copies ran while one was open for 3% of the time, Pallas kernels for 0%

profile of v1, /device:TPU:1, one launch (start us, length us, event | category | flops | bytes accessed | tf_op | source)
XLA Modules:
  0.0 388.9 jit_solution(14033356382578409745)
XLA Ops:
  6.5 0.7 all-gather.5.cloned.1.call-update
  7.3 90.0 %all-gather.5.cloned.1.call-done = bf16[1,1024,3584]{2,1,0:T(8,128)(2,1)} async-done(((bf16[1,128,3584]{2,1,0:T(8,128)(2,1)}), bf16[1,1024,3584]{2,1,0:T(8,128)(2,1)}) %all-gather.5.cloned.1.call-update) | async-done | bytes 7340048 | tf_op jit(solution)/shard_map/all_gather | solution.py:13
  97.3 13.2 %fusion.5 = bf16[1024,1024]{1,0:T(8,128)(2,1)} fusion(bf16[1,3584,1024]{2,1,0:T(8,128)(2,1)} %param.11, bf16[1,1024,3584]{2,1,0:T(8,128)(2,1)} %all-gather.5.cloned.1.call-done), kind=kOutput, calls=%fused_computation.5 | convolution fusion | flops 7517241344 | bytes 16777216 | tf_op jit(solution)/shard_map/dot_general | solution.py:19
  110.5 0.0 all-gather.7.cloned.1.call-start
  110.5 31.0 %reduce-scatter.3.cloned.1.call-done = bf16[256,1024]{1,0:T(8,128)(2,1)} async-done(((bf16[1024,1024]{1,0:T(8,128)(2,1)}), bf16[256,1024]{1,0:T(8,128)(2,1)}) %reduce-scatter.3.cloned.1.call-update) | async-done | bytes 524304 | tf_op jit(solution)/shard_map/reduce_scatter | solution.py:18
  141.5 2.2 all_gather.16
  143.7 0.0 reduce-scatter.5.cloned.1.call-start
  143.8 0.1 copy.15
  143.9 0.1 reduce-window.8
  143.9 0.1 reduce.2
  144.1 6.0 %fusion.2 = f32[1024,32]{0,1:T(8,128)} fusion(bf16[1,1024,3584]{2,1,0:T(8,128)(2,1)} %all-gather.5.cloned.1.call-done, bf16[1,3584,32]{1,2,0:T(8,128)(2,1)S(1)} %copy-done), kind=kOutput, calls=%fused_computation.2 | convolution fusion | flops 234881024 | bytes 7700480 | tf_op jit(solution)/shard_map/dot_general | solution.py:17
  150.2 0.0 all-reduce.5.cloned.1.call-start
  150.2 46.0 %all-gather.7.cloned.1.call-done = f32[2048,1024]{1,0:T(8,128)} async-done(((f32[256,1024]{1,0:T(8,128)}), f32[2048,1024]{1,0:T(8,128)}) %all-gather.7.cloned.1.call-update) | async-done | bytes 8388624 | tf_op jit(solution)/shard_map/all_gather | solution.py:24
  196.2 4.4 %reduce_sum.49 = f32[256,1024]{1,0:T(8,128)S(1)} reduce(f32[8,256,1024]{2,1,0:T(8,128)} %bitcast.25, f32[]{:T(128)} %constant.7.clone.1), dimensions={0}, to_apply=%region_2.0 | reduce | flops 1835008 | bytes 9437188 | tf_op jit(solution)/shard_map/reduce_sum | solution.py:24
  200.6 0.4 multiply_reduce_fusion.1
  201.0 13.9 %all-reduce.1 = (f32[256]{0:T(256)S(1)}, f32[256]{0:T(256)S(1)}) all-reduce(f32[256]{0:T(256)S(1)} %get-tuple-element.6, f32[256]{0:T(256)S(1)} %get-tuple-element.5), channel_id=1, replica_groups=mesh['pipe'=8,'seq'=8,'tensor'=4] {'seq'}, use_global_device_ids=true, to_apply=%region_6.0 | all-reduce | flops 512 | bytes 4096 | tf_op jit(solution)/shard_map/psum | solution.py:27
  214.9 1.2 fusion.10
  216.1 3.4 reduce-scatter.5.cloned.1.call-done
  219.5 0.9 broadcast_multiply_fusion
  220.3 1.3 fusion.19
  221.7 0.6 dynamic-slice
  222.3 139.3 %all-reduce.5.cloned.1.call-done = f32[32,1024]{1,0:T(8,128)} async-done(((f32[32,1024]{1,0:T(8,128)}), f32[32,1024]{1,0:T(8,128)}) %all-reduce.5.cloned.1.call-update) | async-done | bytes 131088
  361.6 2.0 multiply_reduce_fusion.2
  363.6 16.9 %all-reduce.2 = (f32[1]{0:T(128)}, f32[1]{0:T(128)}) all-reduce(f32[1]{0:T(128)} %bitcast.7, f32[1]{0:T(128)} %bitcast.8), channel_id=1, replica_groups=mesh['pipe'=8,'seq'=8,'tensor'=4] {'pipe'}, use_global_device_ids=true, to_apply=%region_10.11 | all-reduce | flops 2 | bytes 16 | tf_op jit(solution)/shard_map/psum | solution.py:51
  (27 shorter events, 0.2 us)
Async XLA Ops:
  6.5 137.5 %copy-start = (bf16[1,3584,32]{1,2,0:T(8,128)(2,1)S(1)}, bf16[1,3584,32]{1,2,0:T(8,128)(2,1)}, u32[]{:S(2)}) copy-start(bf16[1,3584,32]{1,2,0:T(8,128)(2,1)} %param.16) | copy-start | bytes 688132
  6.5 90.8 %all-gather.5.cloned.1.call-start = ((), (), s32[]{:S(2)}) async-start(), calls=%async_computation.4 | async-start | bytes 8257536 | tf_op jit(solution)/shard_map/all_gather | solution.py:13
  7.3 136.5 %copy-start.6 = (s32[32]{0:T(128)S(1)}, s32[32]{0:T(128)}, u32[]{:S(2)}) copy-start(s32[32]{0:T(128)} %param.19) | copy-start | bytes 388
  7.3 134.3 %reduce-scatter.3.cloned.1.call-start = ((), (), s32[]{:S(2)}) async-start(), calls=%async_computation.2 | async-start | bytes 2621440 | tf_op jit(solution)/shard_map/reduce_scatter | solution.py:18
  110.5 85.7 %all-gather.7.cloned.1.call-start = ((), (), s32[]{:S(2)}) async-start(), calls=%async_computation.5 | async-start | bytes 9437184 | tf_op jit(solution)/shard_map/all_gather | solution.py:24
  143.7 75.7 %reduce-scatter.5.cloned.1.call-start = ((), (), s32[]{:S(2)}) async-start(), calls=%async_computation.3 | async-start | bytes 163840 | tf_op jit(solution)/shard_map/reduce_scatter | solution.py:35
  144.1 56.5 %copy-start.1 = (bf16[256,1024]{1,0:T(8,128)(2,1)S(1)}, bf16[256,1024]{1,0:T(8,128)(2,1)}, u32[]{:S(2)}) copy-start(bf16[256,1024]{1,0:T(8,128)(2,1)} %param.13) | copy-start | bytes 1572868
  144.1 56.5 %copy-start.2 = (bf16[256,1024]{1,0:T(8,128)(2,1)S(1)}, bf16[256,1024]{1,0:T(8,128)(2,1)}, u32[]{:S(2)}) copy-start(bf16[256,1024]{1,0:T(8,128)(2,1)} %param.12) | copy-start | bytes 1572868
  144.1 56.5 %copy-start.3 = (f32[1024]{0:T(1024)S(1)}, f32[1024]{0:T(1024)}, u32[]{:S(2)}) copy-start(f32[1024]{0:T(1024)} %param.14) | copy-start | bytes 12292
  150.2 64.7 %copy-start.7 = (f32[1,1024,32]{1,2,0:T(8,128)S(1)}, f32[1,1024,32]{1,2,0:T(8,128)}, u32[]{:S(2)}) copy-start(f32[1,1024,32]{1,2,0:T(8,128)} %param.15) | copy-start | bytes 393220
  150.2 211.4 %all-reduce.5.cloned.1.call-start = ((), (), s32[]{:S(2)}) async-start(), calls=%async_computation.6 | async-start | bytes 262144
  196.2 25.5 %copy-start.8 = (u32[256]{0:T(256)S(1)}, u32[256]{0:T(256)}, u32[]{:S(2)}) copy-start(u32[256]{0:T(256)} %constant.28) | copy-start | bytes 3076
  196.2 165.4 %copy-start.4 = (f32[1,1024]{1,0:T(1,128)S(1)}, f32[1,1024]{1,0:T(1,128)}, u32[]{:S(2)}) copy-start(f32[1,1024]{1,0:T(1,128)} %param.17) | copy-start | bytes 12292
  196.2 165.4 %copy-start.5 = (f32[1,1024]{1,0:T(1,128)S(1)}, f32[1,1024]{1,0:T(1,128)}, u32[]{:S(2)}) copy-start(f32[1,1024]{1,0:T(1,128)} %param.18) | copy-start | bytes 12292
Sparse Core Ops, SparseCore 0:
  9.1 88.0 all-gather.4
  110.6 30.9 reduce-scatter.2
  143.8 52.3 all-gather.6
  198.7 20.7 reduce-scatter.4
  222.8 138.7 all-reduce.4
